TPU v7x, 512 devices: a whole 4x4x16 slice. The times are simulated.
512 devices in a mesh: seq: 16 (over x, y_hi, core), shard: 32 (over y_lo, z).
Axes of the slice: x: 4, y: 4 (y_hi: 2, y_lo: 2; y = y_hi * 2 + y_lo), z: 16, core: 2. Of those that a mesh axis runs over, the one named last changes fastest.
Arguments:
- features: bfloat16 [4096, 4096], P('seq', 'shard'), may hold values from -6 to 6
- in_proj: bfloat16 [4096, 3, 4096], P(None, None, 'shard'), may hold values from -0.09375 to 0.09375
- short_filter: float32 [3, 3, 4096], replicated, may hold values from -3.5 to 3.5
- residue: float32 [16, 4096], P(None, 'shard'), may hold values from -1.5 to 1.5
- decay_rate: float32 [16, 4096], P(None, 'shard'), may hold values from 0.05 to 1000
- skip_gain: float32 [4096], P('shard'), may hold values from -4 to 4
Outputs:
- gated: bfloat16 [4096, 4096], P('seq', 'shard')
All inputs are finite; a program needn't handle non-finite values.
Results may differ from a plain program's by a relative error of at most 0.0063.
Values may be sent and summed in bfloat16 or wider, within the bound.
No kernel may reach another device: no remote copies, remote signals or barrier semaphores. Data moves between devices by JAX's collectives and lax.ppermute only.
A program may use at most 64 MiB of HBM per device.

v0:
```python
import math
import jax
import jax.numpy as jnp
from jax import lax
from jax.sharding import PartitionSpec as P


def shifted(value, axis, steps):
    count = lax.axis_size(axis)
    initial, last = (max(0, -steps), min(count, count - steps))
    return lax.ppermute(value, axis, [(source, source + steps) for source in range(initial, last)])


def mode_tables(residue, decay_rate, total_len, block_len):
    step_rate = decay_rate / total_len
    mode_gain = residue * jnp.sqrt(jnp.expm1(-2.0 * step_rate) / jnp.expm1(-2.0 * decay_rate))
    steps = jnp.arange(block_len, dtype=jnp.float32)[:, None, None]
    lagged = jnp.exp(-step_rate * steps)
    kernel = jnp.sum(mode_gain * lagged, axis=1)
    offsets = jnp.arange(block_len)[:, None] - jnp.arange(block_len)[None, :]
    toeplitz = jnp.where(
        (offsets >= 0)[:, :, None], kernel[jnp.clip(offsets, 0, block_len - 1)], 0.0
    )
    head_table = mode_gain * jnp.exp(-step_rate * (steps + 1.0))
    tail_table = jnp.exp(-step_rate * (block_len - 1.0 - steps))
    step_decay = jnp.exp(-step_rate * block_len)
    return (toeplitz, head_table, tail_table, step_decay)


def project_rows(row_block, w_flat):
    return jnp.dot(
        lax.all_gather(row_block, "shard", axis=1, tiled=True),
        w_flat,
        preferred_element_type=jnp.float32,
    )


def shards(features, in_proj, short_filter, residue, decay_rate, skip_gain):
    length = features.shape[0]
    channels = in_proj.shape[2]
    tap_count = short_filter.shape[0]
    rim_count = tap_count - 1
    seq_count = lax.axis_size("seq")
    total_len = length * seq_count
    w_flat = in_proj.reshape(in_proj.shape[0], 3 * channels)
    proj = project_rows(features, w_flat).astype(jnp.bfloat16).reshape(length, 3, channels)
    rim_rows = shifted(proj[length - rim_count :], "seq", 1)
    extended = jnp.concatenate([rim_rows, proj], 0)
    extended = extended.astype(jnp.float32)
    own_taps = lax.dynamic_slice_in_dim(
        short_filter, lax.axis_index("shard") * channels, channels, 2
    )
    filtered = jnp.zeros((length, 3, channels), jnp.float32)
    for tap_index in range(tap_count):
        start_row = rim_count - tap_index
        filtered = filtered + own_taps[tap_index] * extended[start_row : start_row + length]
    drive_term = filtered[:, 1, :] * filtered[:, 2, :]
    block_len = math.gcd(length, 128)
    block_count = length // block_len
    toeplitz, head_table, tail_table, step_decay = mode_tables(
        residue, decay_rate, total_len, block_len
    )
    highest = lax.Precision.HIGHEST
    blocks = drive_term.reshape(block_count, block_len, channels)
    intra = jnp.einsum("tsc,bsc->btc", toeplitz, blocks, precision=highest)
    states = jnp.einsum("bsc,smc->bmc", blocks, tail_table, precision=highest)

    def accumulate(carried, state_in):
        return (carried * step_decay + state_in, carried)

    total_state, carries = lax.scan(accumulate, jnp.zeros(residue.shape, jnp.float32), states)
    device_decay = jnp.exp(-(decay_rate / total_len) * length)

    def relay(turn, incoming):
        return shifted(incoming * device_decay + total_state, "seq", 1)

    incoming = lax.fori_loop(0, seq_count - 1, relay, jnp.zeros_like(total_state))
    block_starts = (block_len * jnp.arange(block_count, dtype=jnp.float32))[:, None, None]
    entering = carries + jnp.exp(-(decay_rate / total_len)[None] * block_starts) * incoming[None]
    correction = jnp.einsum("tmc,bmc->btc", head_table, entering, precision=highest)
    longconv = (intra + correction).reshape(length, channels)
    return (filtered[:, 0, :] * (longconv + skip_gain * drive_term)).astype(jnp.bfloat16)


def solution(mesh):
    placed = (
        P("seq", "shard"),
        P(None, None, "shard"),
        P(),
        P(None, "shard"),
        P(None, "shard"),
        P("shard"),
    )
    return jax.shard_map(
        shards, mesh=mesh, in_specs=placed, out_specs=P("seq", "shard"), check_vma=False
    )
```

profile of v0, /device:TPU:2, one launch (start us, length us, event | category | flops | bytes accessed | tf_op | source)
XLA Modules:
  0.0 349.9 jit_solution(4702001722327481454)
XLA Ops:
  6.5 0.7 all-gather.2.cloned.1.call-update
  7.3 3.2 copy.26
  10.5 0.7 sqrt_multiply_fusion
  11.5 0.7 dynamic-slice_bitcast_fusion.2
  12.2 1.2 multiply_reduce_fusion
  13.5 128.5 %all-gather.2.cloned.1.call-done = bf16[256,4096]{1,0:T(8,128)(2,1)} async-done(((bf16[256,128]{1,0:T(8,128)(2,1)}), bf16[256,4096]{1,0:T(8,128)(2,1)}) %all-gather.2.cloned.1.call-update) | async-done | bytes 2097168 | tf_op jit(solution)/shard_map/all_gather | solution.py:32
  142.0 2.9 convolution_convert_fusion
  144.9 1.9 collective-permute-start.1
  146.8 0.9 copy.31
  147.8 54.5 %gather_fusion = f32[16384,128]{1,0:T(8,128)} fusion(f32[128,128]{1,0:T(8,128)S(1)} %copy.31, s32[16384]{0:T(1024)S(1)} %fusion.23), kind=kCustom, calls=%fused_computation | custom fusion | bytes 16842752 | tf_op jit(solution)/shard_map/gather | solution.py:22
  202.3 9.4 %copy.32 = f32[128,128,128]{1,0,2:T(8,128)} copy(f32[128,128,128]{2,1,0:T(8,128)} %bitcast.48) | data formatting | bytes 16777216 | tf_op jit(solution)/shard_map/gather | solution.py:22
  211.8 0.2 copy.28
  212.1 0.4 fusion.18
  212.7 1.9 convolution_bitcast_fusion
  214.7 110.5 %while.23 = (s32[]{:T(128)}, f32[16,128]{1,0:T(8,128)S(1)}, f32[16,128]{1,0:T(8,128)S(1)}, f32[16,128]{1,0:T(8,128)S(1)}, s32[]{:T(128)}) while((s32[]{:T(128)}, f32[16,128]{1,0:T(8,128)S(1)}, f32[16,128]{1,0:T(8,128)S(1)}, f32[16,128]{1,0:T(8,128)S(1)}, s32[]{:T(128)}) %tuple.46), condition=%wide.region_4.5_spmd, body=%wide.region_3.4_spmd.sunk | while | flops 4098 | bytes 65637 | solution.py:77
  214.7 5.1 %collective-permute-start = (f32[16,128]{1,0:T(8,128)S(1)}, f32[16,128]{1,0:T(8,128)S(1)}, u32[]{:S(2)}, u32[]{:S(2)}) collective-permute-start(f32[16,128]{1,0:T(8,128)S(1)} %multiply_add_fusion.3), channel_id=1, source_target_pairs={{0,32},{32,64},{64,96},{96,128},{128,160},{160,192},{192,224},{224... | collective-permute-start | bytes 24584 | tf_op jit(solution)/shard_map/while/body/eval_jaxpr/ppermute | solution.py:11
  219.9 2.2 collective-permute-done
  222.1 1.9 collective-permute-start
  224.0 5.4 %collective-permute-done = f32[16,128]{1,0:T(8,128)S(1)} collective-permute-done((f32[16,128]{1,0:T(8,128)S(1)}, f32[16,128]{1,0:T(8,128)S(1)}, u32[]{:S(2)}, u32[]{:S(2)}) %collective-permute-start) | collective-permute-done | bytes 8224 | tf_op jit(solution)/shard_map/while/body/eval_jaxpr/ppermute | solution.py:11
  229.5 1.9 collective-permute-start
  231.4 5.4 %collective-permute-done = f32[16,128]{1,0:T(8,128)S(1)} collective-permute-done((f32[16,128]{1,0:T(8,128)S(1)}, f32[16,128]{1,0:T(8,128)S(1)}, u32[]{:S(2)}, u32[]{:S(2)}) %collective-permute-start) | collective-permute-done | bytes 8224 | tf_op jit(solution)/shard_map/while/body/eval_jaxpr/ppermute | solution.py:11
  236.8 1.9 collective-permute-start
  238.8 5.4 %collective-permute-done = f32[16,128]{1,0:T(8,128)S(1)} collective-permute-done((f32[16,128]{1,0:T(8,128)S(1)}, f32[16,128]{1,0:T(8,128)S(1)}, u32[]{:S(2)}, u32[]{:S(2)}) %collective-permute-start) | collective-permute-done | bytes 8224 | tf_op jit(solution)/shard_map/while/body/eval_jaxpr/ppermute | solution.py:11
  244.2 1.9 collective-permute-start
  246.1 5.4 %collective-permute-done = f32[16,128]{1,0:T(8,128)S(1)} collective-permute-done((f32[16,128]{1,0:T(8,128)S(1)}, f32[16,128]{1,0:T(8,128)S(1)}, u32[]{:S(2)}, u32[]{:S(2)}) %collective-permute-start) | collective-permute-done | bytes 8224 | tf_op jit(solution)/shard_map/while/body/eval_jaxpr/ppermute | solution.py:11
  251.6 1.9 collective-permute-start
  253.5 5.4 %collective-permute-done = f32[16,128]{1,0:T(8,128)S(1)} collective-permute-done((f32[16,128]{1,0:T(8,128)S(1)}, f32[16,128]{1,0:T(8,128)S(1)}, u32[]{:S(2)}, u32[]{:S(2)}) %collective-permute-start) | collective-permute-done | bytes 8224 | tf_op jit(solution)/shard_map/while/body/eval_jaxpr/ppermute | solution.py:11
  258.9 1.9 collective-permute-start
  260.9 5.4 %collective-permute-done = f32[16,128]{1,0:T(8,128)S(1)} collective-permute-done((f32[16,128]{1,0:T(8,128)S(1)}, f32[16,128]{1,0:T(8,128)S(1)}, u32[]{:S(2)}, u32[]{:S(2)}) %collective-permute-start) | collective-permute-done | bytes 8224 | tf_op jit(solution)/shard_map/while/body/eval_jaxpr/ppermute | solution.py:11
  266.3 1.9 collective-permute-start
  268.2 5.4 %collective-permute-done = f32[16,128]{1,0:T(8,128)S(1)} collective-permute-done((f32[16,128]{1,0:T(8,128)S(1)}, f32[16,128]{1,0:T(8,128)S(1)}, u32[]{:S(2)}, u32[]{:S(2)}) %collective-permute-start) | collective-permute-done | bytes 8224 | tf_op jit(solution)/shard_map/while/body/eval_jaxpr/ppermute | solution.py:11
  273.7 1.9 collective-permute-start
  275.6 5.4 %collective-permute-done = f32[16,128]{1,0:T(8,128)S(1)} collective-permute-done((f32[16,128]{1,0:T(8,128)S(1)}, f32[16,128]{1,0:T(8,128)S(1)}, u32[]{:S(2)}, u32[]{:S(2)}) %collective-permute-start) | collective-permute-done | bytes 8224 | tf_op jit(solution)/shard_map/while/body/eval_jaxpr/ppermute | solution.py:11
  281.0 1.9 collective-permute-start
  283.0 5.4 %collective-permute-done = f32[16,128]{1,0:T(8,128)S(1)} collective-permute-done((f32[16,128]{1,0:T(8,128)S(1)}, f32[16,128]{1,0:T(8,128)S(1)}, u32[]{:S(2)}, u32[]{:S(2)}) %collective-permute-start) | collective-permute-done | bytes 8224 | tf_op jit(solution)/shard_map/while/body/eval_jaxpr/ppermute | solution.py:11
  288.4 1.9 collective-permute-start
  290.3 5.4 %collective-permute-done = f32[16,128]{1,0:T(8,128)S(1)} collective-permute-done((f32[16,128]{1,0:T(8,128)S(1)}, f32[16,128]{1,0:T(8,128)S(1)}, u32[]{:S(2)}, u32[]{:S(2)}) %collective-permute-start) | collective-permute-done | bytes 8224 | tf_op jit(solution)/shard_map/while/body/eval_jaxpr/ppermute | solution.py:11
  295.8 1.9 collective-permute-start
  297.7 5.4 %collective-permute-done = f32[16,128]{1,0:T(8,128)S(1)} collective-permute-done((f32[16,128]{1,0:T(8,128)S(1)}, f32[16,128]{1,0:T(8,128)S(1)}, u32[]{:S(2)}, u32[]{:S(2)}) %collective-permute-start) | collective-permute-done | bytes 8224 | tf_op jit(solution)/shard_map/while/body/eval_jaxpr/ppermute | solution.py:11
  303.1 1.9 collective-permute-start
  305.1 5.4 %collective-permute-done = f32[16,128]{1,0:T(8,128)S(1)} collective-permute-done((f32[16,128]{1,0:T(8,128)S(1)}, f32[16,128]{1,0:T(8,128)S(1)}, u32[]{:S(2)}, u32[]{:S(2)}) %collective-permute-start) | collective-permute-done | bytes 8224 | tf_op jit(solution)/shard_map/while/body/eval_jaxpr/ppermute | solution.py:11
  310.5 1.9 collective-permute-start
  312.4 5.4 %collective-permute-done = f32[16,128]{1,0:T(8,128)S(1)} collective-permute-done((f32[16,128]{1,0:T(8,128)S(1)}, f32[16,128]{1,0:T(8,128)S(1)}, u32[]{:S(2)}, u32[]{:S(2)}) %collective-permute-start) | collective-permute-done | bytes 8224 | tf_op jit(solution)/shard_map/while/body/eval_jaxpr/ppermute | solution.py:11
  317.9 1.9 collective-permute-start
  319.8 5.4 %collective-permute-done = f32[16,128]{1,0:T(8,128)S(1)} collective-permute-done((f32[16,128]{1,0:T(8,128)S(1)}, f32[16,128]{1,0:T(8,128)S(1)}, u32[]{:S(2)}, u32[]{:S(2)}) %collective-permute-start) | collective-permute-done | bytes 8224 | tf_op jit(solution)/shard_map/while/body/eval_jaxpr/ppermute | solution.py:11
  325.4 1.4 fusion.7
  326.8 15.4 %fusion.4 = f32[128,2,128]{2,1,0:T(2,128)S(1)} fusion(f32[128,2,128]{2,1,0:T(2,128)S(1)} %fusion.7, f32[2,128,128]{1,0,2:T(2,128)S(1)} %mul.171, f32[128,128,128]{1,0,2:T(8,128)} %copy.32, pred[128,128]{1,0:T(8,128)(4,1)S(1)} %subtract_compare_fusion), kind=kOutput, calls=%fused_computation.9 | convolution fusion | flops 52461568 | bytes 8798208 | tf_op jit(solution)/shard_map/tsc,bsc->btc/dot_general | solution.py:65
  342.4 0.7 copy.35
  (48 shorter events, 1.3 us)
Async XLA Ops:
  6.5 135.4 %all-gather.2.cloned.1.call-start = ((), (), s32[]{:S(2)}) async-start(), calls=%async_computation | async-start | bytes 2162688 | tf_op jit(solution)/shard_map/all_gather | solution.py:32
  11.4 0.8 copy-start
  144.9 66.9 %collective-permute-start.1 = (bf16[2,3,128]{2,1,0:T(4,128)(2,1)S(1)}, bf16[2,3,128]{2,1,0:T(4,128)(2,1)S(1)}, u32[]{:S(2)}, u32[]{:S(2)}) collective-permute-start(bf16[2,3,128]{2,1,0:T(4,128)(2,1)S(1)} %slice.35), channel_id=1, source_target_pairs={{0,32},{32,64},{64,96},{96,128},{128,160},{160,192},{192,224},{224... | collective-permute-start | bytes 4616 | tf_op jit(solution)/shard_map/ppermute | solution.py:11
  202.3 123.2 %copy-start.1 = (f32[16,128]{0,1:T(8,128)S(1)}, f32[16,128]{0,1:T(8,128)}, u32[]{:S(2)}) copy-start(f32[16,128]{0,1:T(8,128)} %copy-done) | copy-start | bytes 24580
  211.6 130.6 %copy-start.2 = (f32[128]{0:T(128)S(1)}, f32[128]{0:T(128)}, u32[]{:S(2)}) copy-start(f32[128]{0:T(128)} %param.15) | copy-start | bytes 1540
  214.7 7.4 %collective-permute-start = (f32[16,128]{1,0:T(8,128)S(1)}, f32[16,128]{1,0:T(8,128)S(1)}, u32[]{:S(2)}, u32[]{:S(2)}) collective-permute-start(f32[16,128]{1,0:T(8,128)S(1)} %multiply_add_fusion.3), channel_id=1, source_target_pairs={{0,32},{32,64},{64,96},{96,128},{128,160},{160,192},{192,224},{224... | collective-permute-start | bytes 24584 | tf_op jit(solution)/shard_map/while/body/eval_jaxpr/ppermute | solution.py:11
  222.1 7.4 %collective-permute-start = (f32[16,128]{1,0:T(8,128)S(1)}, f32[16,128]{1,0:T(8,128)S(1)}, u32[]{:S(2)}, u32[]{:S(2)}) collective-permute-start(f32[16,128]{1,0:T(8,128)S(1)} %multiply_add_fusion.3), channel_id=1, source_target_pairs={{0,32},{32,64},{64,96},{96,128},{128,160},{160,192},{192,224},{224... | collective-permute-start | bytes 24584 | tf_op jit(solution)/shard_map/while/body/eval_jaxpr/ppermute | solution.py:11
  229.5 7.4 %collective-permute-start = (f32[16,128]{1,0:T(8,128)S(1)}, f32[16,128]{1,0:T(8,128)S(1)}, u32[]{:S(2)}, u32[]{:S(2)}) collective-permute-start(f32[16,128]{1,0:T(8,128)S(1)} %multiply_add_fusion.3), channel_id=1, source_target_pairs={{0,32},{32,64},{64,96},{96,128},{128,160},{160,192},{192,224},{224... | collective-permute-start | bytes 24584 | tf_op jit(solution)/shard_map/while/body/eval_jaxpr/ppermute | solution.py:11
  236.8 7.4 %collective-permute-start = (f32[16,128]{1,0:T(8,128)S(1)}, f32[16,128]{1,0:T(8,128)S(1)}, u32[]{:S(2)}, u32[]{:S(2)}) collective-permute-start(f32[16,128]{1,0:T(8,128)S(1)} %multiply_add_fusion.3), channel_id=1, source_target_pairs={{0,32},{32,64},{64,96},{96,128},{128,160},{160,192},{192,224},{224... | collective-permute-start | bytes 24584 | tf_op jit(solution)/shard_map/while/body/eval_jaxpr/ppermute | solution.py:11
  244.2 7.4 %collective-permute-start = (f32[16,128]{1,0:T(8,128)S(1)}, f32[16,128]{1,0:T(8,128)S(1)}, u32[]{:S(2)}, u32[]{:S(2)}) collective-permute-start(f32[16,128]{1,0:T(8,128)S(1)} %multiply_add_fusion.3), channel_id=1, source_target_pairs={{0,32},{32,64},{64,96},{96,128},{128,160},{160,192},{192,224},{224... | collective-permute-start | bytes 24584 | tf_op jit(solution)/shard_map/while/body/eval_jaxpr/ppermute | solution.py:11
  251.6 7.4 %collective-permute-start = (f32[16,128]{1,0:T(8,128)S(1)}, f32[16,128]{1,0:T(8,128)S(1)}, u32[]{:S(2)}, u32[]{:S(2)}) collective-permute-start(f32[16,128]{1,0:T(8,128)S(1)} %multiply_add_fusion.3), channel_id=1, source_target_pairs={{0,32},{32,64},{64,96},{96,128},{128,160},{160,192},{192,224},{224... | collective-permute-start | bytes 24584 | tf_op jit(solution)/shard_map/while/body/eval_jaxpr/ppermute | solution.py:11
  258.9 7.4 %collective-permute-start = (f32[16,128]{1,0:T(8,128)S(1)}, f32[16,128]{1,0:T(8,128)S(1)}, u32[]{:S(2)}, u32[]{:S(2)}) collective-permute-start(f32[16,128]{1,0:T(8,128)S(1)} %multiply_add_fusion.3), channel_id=1, source_target_pairs={{0,32},{32,64},{64,96},{96,128},{128,160},{160,192},{192,224},{224... | collective-permute-start | bytes 24584 | tf_op jit(solution)/shard_map/while/body/eval_jaxpr/ppermute | solution.py:11
  266.3 7.4 %collective-permute-start = (f32[16,128]{1,0:T(8,128)S(1)}, f32[16,128]{1,0:T(8,128)S(1)}, u32[]{:S(2)}, u32[]{:S(2)}) collective-permute-start(f32[16,128]{1,0:T(8,128)S(1)} %multiply_add_fusion.3), channel_id=1, source_target_pairs={{0,32},{32,64},{64,96},{96,128},{128,160},{160,192},{192,224},{224... | collective-permute-start | bytes 24584 | tf_op jit(solution)/shard_map/while/body/eval_jaxpr/ppermute | solution.py:11
  273.7 7.4 %collective-permute-start = (f32[16,128]{1,0:T(8,128)S(1)}, f32[16,128]{1,0:T(8,128)S(1)}, u32[]{:S(2)}, u32[]{:S(2)}) collective-permute-start(f32[16,128]{1,0:T(8,128)S(1)} %multiply_add_fusion.3), channel_id=1, source_target_pairs={{0,32},{32,64},{64,96},{96,128},{128,160},{160,192},{192,224},{224... | collective-permute-start | bytes 24584 | tf_op jit(solution)/shard_map/while/body/eval_jaxpr/ppermute | solution.py:11
  281.0 7.4 %collective-permute-start = (f32[16,128]{1,0:T(8,128)S(1)}, f32[16,128]{1,0:T(8,128)S(1)}, u32[]{:S(2)}, u32[]{:S(2)}) collective-permute-start(f32[16,128]{1,0:T(8,128)S(1)} %multiply_add_fusion.3), channel_id=1, source_target_pairs={{0,32},{32,64},{64,96},{96,128},{128,160},{160,192},{192,224},{224... | collective-permute-start | bytes 24584 | tf_op jit(solution)/shard_map/while/body/eval_jaxpr/ppermute | solution.py:11
  288.4 7.4 %collective-permute-start = (f32[16,128]{1,0:T(8,128)S(1)}, f32[16,128]{1,0:T(8,128)S(1)}, u32[]{:S(2)}, u32[]{:S(2)}) collective-permute-start(f32[16,128]{1,0:T(8,128)S(1)} %multiply_add_fusion.3), channel_id=1, source_target_pairs={{0,32},{32,64},{64,96},{96,128},{128,160},{160,192},{192,224},{224... | collective-permute-start | bytes 24584 | tf_op jit(solution)/shard_map/while/body/eval_jaxpr/ppermute | solution.py:11
  295.8 7.4 %collective-permute-start = (f32[16,128]{1,0:T(8,128)S(1)}, f32[16,128]{1,0:T(8,128)S(1)}, u32[]{:S(2)}, u32[]{:S(2)}) collective-permute-start(f32[16,128]{1,0:T(8,128)S(1)} %multiply_add_fusion.3), channel_id=1, source_target_pairs={{0,32},{32,64},{64,96},{96,128},{128,160},{160,192},{192,224},{224... | collective-permute-start | bytes 24584 | tf_op jit(solution)/shard_map/while/body/eval_jaxpr/ppermute | solution.py:11
  303.1 7.4 %collective-permute-start = (f32[16,128]{1,0:T(8,128)S(1)}, f32[16,128]{1,0:T(8,128)S(1)}, u32[]{:S(2)}, u32[]{:S(2)}) collective-permute-start(f32[16,128]{1,0:T(8,128)S(1)} %multiply_add_fusion.3), channel_id=1, source_target_pairs={{0,32},{32,64},{64,96},{96,128},{128,160},{160,192},{192,224},{224... | collective-permute-start | bytes 24584 | tf_op jit(solution)/shard_map/while/body/eval_jaxpr/ppermute | solution.py:11
  310.5 7.4 %collective-permute-start = (f32[16,128]{1,0:T(8,128)S(1)}, f32[16,128]{1,0:T(8,128)S(1)}, u32[]{:S(2)}, u32[]{:S(2)}) collective-permute-start(f32[16,128]{1,0:T(8,128)S(1)} %multiply_add_fusion.3), channel_id=1, source_target_pairs={{0,32},{32,64},{64,96},{96,128},{128,160},{160,192},{192,224},{224... | collective-permute-start | bytes 24584 | tf_op jit(solution)/shard_map/while/body/eval_jaxpr/ppermute | solution.py:11
  317.9 7.4 %collective-permute-start = (f32[16,128]{1,0:T(8,128)S(1)}, f32[16,128]{1,0:T(8,128)S(1)}, u32[]{:S(2)}, u32[]{:S(2)}) collective-permute-start(f32[16,128]{1,0:T(8,128)S(1)} %multiply_add_fusion.3), channel_id=1, source_target_pairs={{0,32},{32,64},{64,96},{96,128},{128,160},{160,192},{192,224},{224... | collective-permute-start | bytes 24584 | tf_op jit(solution)/shard_map/while/body/eval_jaxpr/ppermute | solution.py:11
Sparse Core Ops, SparseCore 0:
  9.4 132.5 all-gather.1
where the time goes:
time: 351 us; the launch traced here: 350 us
  waiting for transfers between devices  208 us (59%)
  local copies, waits for them, and re-layouts  70.3 us (20%)
  starting transfers between devices  33.8 us (10%)
  matrix products  21.5 us (6%)
  between operations  13.6 us (4%)
    all_gather x1, waiting for transfers between devices, project_rows(): lax.all_gather(row_block, 'shard', axis=1, tiled=True)  128 us
    ppermute x16, waiting for transfers between devices, shifted(): lax.ppermute(value, axis, [(source, source + steps) for source in range(i...  78.4 us
    gather x2, local copies, waits for them, and re-layouts, mode_tables(): kernel[jnp.clip(offsets, 0, block_len - 1)]  63.9 us
    ppermute x16, starting transfers between devices, shifted(): lax.ppermute(value, axis, [(source, source + steps) for source in range(i...  33.8 us
    dot_general x1, matrix products, shards(): intra = jnp.einsum('tsc,bsc->btc', toeplitz, blocks, precision=highest)  15.4 us
  transfers between devices with their start and end apart: 17, of which 16 were waited for; matrix products, arithmetic and copies ran while one was open for 20% of the time, Pallas kernels for 0%

commit v1 on v0

--- a/solution.py
+++ b/solution.py
@@ -29,7 +29,9 @@
 
 def project_rows(row_block, w_flat):
     return jnp.dot(
-        lax.all_gather(row_block, "shard", axis=1, tiled=True),
+        jnp.concatenate(
+            lax.all_to_all(jnp.stack([row_block] * lax.axis_size("shard")), "shard", 0, 0), axis=1
+        ),
         w_flat,
         preferred_element_type=jnp.float32,
     )

time: 351 us -> 321 us (0.915)
  the two profiles are of different devices: /device:TPU:2 before, /device:TPU:38 now
where the time goes in v1:
time: 321 us; the launch traced here: 320 us
  waiting for transfers between devices  174 us (54%)
  local copies, waits for them, and re-layouts  71.6 us (22%)
  starting transfers between devices  50.3 us (16%)
  matrix products  22.5 us (7%)
    all_to_all x1, waiting for transfers between devices, project_rows(): lax.all_to_all(jnp.stack([row_block] * lax.axis_size('shard')), 'shard',...  95.4 us
    ppermute x16, waiting for transfers between devices, shifted(): lax.ppermute(value, axis, [(source, source + steps) for source in range(i...  78.6 us
    gather x2, local copies, waits for them, and re-layouts, mode_tables(): kernel[jnp.clip(offsets, 0, block_len - 1)]  63.8 us
    ppermute x16, starting transfers between devices, shifted(): lax.ppermute(value, axis, [(source, source + steps) for source in range(i...  33.7 us
    all_to_all x1, starting transfers between devices, project_rows(): lax.all_to_all(jnp.stack([row_block] * lax.axis_size('shard')), 'shard',...  16.6 us
    dot_general x1, matrix products, shards(): intra = jnp.einsum('tsc,bsc->btc', toeplitz, blocks, precision=highest)  15.4 us
  transfers between devices with their start and end apart: 17, of which 16 were waited for; matrix products, arithmetic and copies ran while one was open for 21% of the time, Pallas kernels for 0%

profile of v1, /device:TPU:38, one launch (start us, length us, event | category | flops | bytes accessed | tf_op | source)
XLA Modules:
  0.0 320.5 jit_solution(18287305164412612240)
XLA Ops:
  0.0 0.9 copy.27
  1.0 1.6 stack.2
  2.5 16.6 %all-to-all-start = ((bf16[32,256,128]{1,2,0:T(8,128)(2,1)}), bf16[32,256,128]{1,2,0:T(8,128)(2,1)}, u32[]{:S(2)}, u32[]{:S(2)}) async-start(bf16[32,256,128]{1,2,0:T(8,128)(2,1)} %stack.2), calls=%async_computation | async-start | bytes 4194304 | tf_op jit(solution)/shard_map/all_to_all | solution.py:33
  19.1 2.8 copy.28
  22.2 0.7 dynamic-slice_bitcast_fusion.2
  23.0 0.6 multiply_reduce_fusion
  23.7 95.4 %all-to-all-done = bf16[32,256,128]{1,2,0:T(8,128)(2,1)} async-done(((bf16[32,256,128]{1,2,0:T(8,128)(2,1)}), bf16[32,256,128]{1,2,0:T(8,128)(2,1)}, u32[]{:S(2)}, u32[]{:S(2)}) %all-to-all-start) | async-done | bytes 2097184 | tf_op jit(solution)/shard_map/all_to_all | solution.py:33
  119.1 3.8 %convolution_convert_fusion = bf16[256,384]{1,0:T(8,128)(2,1)S(1)} fusion(bf16[256,4096]{0,1:T(8,128)(2,1)} %bitcast.2, bf16[4096,384]{0,1:T(8,128)(2,1)} %bitcast.52), kind=kOutput, calls=%fused_computation.8 | convolution fusion | flops 805404672 | bytes 5439488 | tf_op jit(solution)/shard_map/dot_general | solution.py:31
  123.0 2.1 collective-permute-start.1
  125.2 54.5 %gather_fusion = f32[16384,128]{1,0:T(8,128)} fusion(f32[128,128]{1,0:T(8,128)S(1)} %copy.33, s32[16384]{0:T(1024)S(1)} %fusion.23), kind=kCustom, calls=%fused_computation | custom fusion | bytes 16842752 | tf_op jit(solution)/shard_map/gather | solution.py:22
  179.7 9.3 %copy.34 = f32[128,128,128]{1,0,2:T(8,128)} copy(f32[128,128,128]{2,1,0:T(8,128)} %bitcast.51) | data formatting | bytes 16777216 | tf_op jit(solution)/shard_map/gather | solution.py:22
  189.2 0.2 copy.30
  189.5 0.4 fusion.18
  190.1 1.9 convolution_bitcast_fusion
  192.1 110.5 %while.23 = (s32[]{:T(128)}, f32[16,128]{1,0:T(8,128)S(1)}, f32[16,128]{1,0:T(8,128)S(1)}, f32[16,128]{1,0:T(8,128)S(1)}, s32[]{:T(128)}) while((s32[]{:T(128)}, f32[16,128]{1,0:T(8,128)S(1)}, f32[16,128]{1,0:T(8,128)S(1)}, f32[16,128]{1,0:T(8,128)S(1)}, s32[]{:T(128)}) %tuple.46), condition=%wide.region_4.5_spmd, body=%wide.region_3.4_spmd.sunk | while | flops 4098 | bytes 65637 | solution.py:79
  192.1 4.9 %collective-permute-start = (f32[16,128]{1,0:T(8,128)S(1)}, f32[16,128]{1,0:T(8,128)S(1)}, u32[]{:S(2)}, u32[]{:S(2)}) collective-permute-start(f32[16,128]{1,0:T(8,128)S(1)} %multiply_add_fusion.3), channel_id=1, source_target_pairs={{0,32},{32,64},{64,96},{96,128},{128,160},{160,192},{192,224},{224... | collective-permute-start | bytes 24584 | tf_op jit(solution)/shard_map/while/body/eval_jaxpr/ppermute | solution.py:11
  197.0 2.5 collective-permute-done
  199.5 1.9 collective-permute-start
  201.4 5.4 %collective-permute-done = f32[16,128]{1,0:T(8,128)S(1)} collective-permute-done((f32[16,128]{1,0:T(8,128)S(1)}, f32[16,128]{1,0:T(8,128)S(1)}, u32[]{:S(2)}, u32[]{:S(2)}) %collective-permute-start) | collective-permute-done | bytes 8224 | tf_op jit(solution)/shard_map/while/body/eval_jaxpr/ppermute | solution.py:11
  206.9 1.9 collective-permute-start
  208.8 5.4 %collective-permute-done = f32[16,128]{1,0:T(8,128)S(1)} collective-permute-done((f32[16,128]{1,0:T(8,128)S(1)}, f32[16,128]{1,0:T(8,128)S(1)}, u32[]{:S(2)}, u32[]{:S(2)}) %collective-permute-start) | collective-permute-done | bytes 8224 | tf_op jit(solution)/shard_map/while/body/eval_jaxpr/ppermute | solution.py:11
  214.2 1.9 collective-permute-start
  216.1 5.4 %collective-permute-done = f32[16,128]{1,0:T(8,128)S(1)} collective-permute-done((f32[16,128]{1,0:T(8,128)S(1)}, f32[16,128]{1,0:T(8,128)S(1)}, u32[]{:S(2)}, u32[]{:S(2)}) %collective-permute-start) | collective-permute-done | bytes 8224 | tf_op jit(solution)/shard_map/while/body/eval_jaxpr/ppermute | solution.py:11
  221.6 1.9 collective-permute-start
  223.5 5.4 %collective-permute-done = f32[16,128]{1,0:T(8,128)S(1)} collective-permute-done((f32[16,128]{1,0:T(8,128)S(1)}, f32[16,128]{1,0:T(8,128)S(1)}, u32[]{:S(2)}, u32[]{:S(2)}) %collective-permute-start) | collective-permute-done | bytes 8224 | tf_op jit(solution)/shard_map/while/body/eval_jaxpr/ppermute | solution.py:11
  229.0 1.9 collective-permute-start
  230.9 5.4 %collective-permute-done = f32[16,128]{1,0:T(8,128)S(1)} collective-permute-done((f32[16,128]{1,0:T(8,128)S(1)}, f32[16,128]{1,0:T(8,128)S(1)}, u32[]{:S(2)}, u32[]{:S(2)}) %collective-permute-start) | collective-permute-done | bytes 8224 | tf_op jit(solution)/shard_map/while/body/eval_jaxpr/ppermute | solution.py:11
  236.3 1.9 collective-permute-start
  238.2 5.4 %collective-permute-done = f32[16,128]{1,0:T(8,128)S(1)} collective-permute-done((f32[16,128]{1,0:T(8,128)S(1)}, f32[16,128]{1,0:T(8,128)S(1)}, u32[]{:S(2)}, u32[]{:S(2)}) %collective-permute-start) | collective-permute-done | bytes 8224 | tf_op jit(solution)/shard_map/while/body/eval_jaxpr/ppermute | solution.py:11
  243.7 1.9 collective-permute-start
  245.6 5.4 %collective-permute-done = f32[16,128]{1,0:T(8,128)S(1)} collective-permute-done((f32[16,128]{1,0:T(8,128)S(1)}, f32[16,128]{1,0:T(8,128)S(1)}, u32[]{:S(2)}, u32[]{:S(2)}) %collective-permute-start) | collective-permute-done | bytes 8224 | tf_op jit(solution)/shard_map/while/body/eval_jaxpr/ppermute | solution.py:11
  251.1 1.9 collective-permute-start
  253.0 5.4 %collective-permute-done = f32[16,128]{1,0:T(8,128)S(1)} collective-permute-done((f32[16,128]{1,0:T(8,128)S(1)}, f32[16,128]{1,0:T(8,128)S(1)}, u32[]{:S(2)}, u32[]{:S(2)}) %collective-permute-start) | collective-permute-done | bytes 8224 | tf_op jit(solution)/shard_map/while/body/eval_jaxpr/ppermute | solution.py:11
  258.4 1.9 collective-permute-start
  260.3 5.4 %collective-permute-done = f32[16,128]{1,0:T(8,128)S(1)} collective-permute-done((f32[16,128]{1,0:T(8,128)S(1)}, f32[16,128]{1,0:T(8,128)S(1)}, u32[]{:S(2)}, u32[]{:S(2)}) %collective-permute-start) | collective-permute-done | bytes 8224 | tf_op jit(solution)/shard_map/while/body/eval_jaxpr/ppermute | solution.py:11
  265.8 1.9 collective-permute-start
  267.7 5.4 %collective-permute-done = f32[16,128]{1,0:T(8,128)S(1)} collective-permute-done((f32[16,128]{1,0:T(8,128)S(1)}, f32[16,128]{1,0:T(8,128)S(1)}, u32[]{:S(2)}, u32[]{:S(2)}) %collective-permute-start) | collective-permute-done | bytes 8224 | tf_op jit(solution)/shard_map/while/body/eval_jaxpr/ppermute | solution.py:11
  273.2 1.9 collective-permute-start
  275.1 5.4 %collective-permute-done = f32[16,128]{1,0:T(8,128)S(1)} collective-permute-done((f32[16,128]{1,0:T(8,128)S(1)}, f32[16,128]{1,0:T(8,128)S(1)}, u32[]{:S(2)}, u32[]{:S(2)}) %collective-permute-start) | collective-permute-done | bytes 8224 | tf_op jit(solution)/shard_map/while/body/eval_jaxpr/ppermute | solution.py:11
  280.5 1.9 collective-permute-start
  282.4 5.4 %collective-permute-done = f32[16,128]{1,0:T(8,128)S(1)} collective-permute-done((f32[16,128]{1,0:T(8,128)S(1)}, f32[16,128]{1,0:T(8,128)S(1)}, u32[]{:S(2)}, u32[]{:S(2)}) %collective-permute-start) | collective-permute-done | bytes 8224 | tf_op jit(solution)/shard_map/while/body/eval_jaxpr/ppermute | solution.py:11
  287.9 1.9 collective-permute-start
  289.8 5.4 %collective-permute-done = f32[16,128]{1,0:T(8,128)S(1)} collective-permute-done((f32[16,128]{1,0:T(8,128)S(1)}, f32[16,128]{1,0:T(8,128)S(1)}, u32[]{:S(2)}, u32[]{:S(2)}) %collective-permute-start) | collective-permute-done | bytes 8224 | tf_op jit(solution)/shard_map/while/body/eval_jaxpr/ppermute | solution.py:11
  295.3 1.9 collective-permute-start
  297.2 5.4 %collective-permute-done = f32[16,128]{1,0:T(8,128)S(1)} collective-permute-done((f32[16,128]{1,0:T(8,128)S(1)}, f32[16,128]{1,0:T(8,128)S(1)}, u32[]{:S(2)}, u32[]{:S(2)}) %collective-permute-start) | collective-permute-done | bytes 8224 | tf_op jit(solution)/shard_map/while/body/eval_jaxpr/ppermute | solution.py:11
  302.8 1.4 fusion.7
  304.2 15.4 %fusion.4 = f32[128,2,128]{2,1,0:T(2,128)S(1)} fusion(f32[128,2,128]{2,1,0:T(2,128)S(1)} %fusion.7, f32[2,128,128]{1,0,2:T(2,128)S(1)} %mul.171, f32[128,128,128]{1,0,2:T(8,128)} %copy.34, pred[128,128]{1,0:T(8,128)(4,1)S(1)} %subtract_compare_fusion), kind=kOutput, calls=%fused_computation.9 | convolution fusion | flops 52461568 | bytes 8798208 | tf_op jit(solution)/shard_map/tsc,bsc->btc/dot_general | solution.py:67
  319.8 0.7 copy.37
  (51 shorter events, 1.4 us)
Async XLA Ops:
  0.9 18.2 %copy-start = (bf16[4096,3,128]{2,0,1:T(8,128)(2,1)S(1)}, bf16[4096,3,128]{2,0,1:T(8,128)(2,1)}, u32[]{:S(2)}) copy-start(bf16[4096,3,128]{2,0,1:T(8,128)(2,1)} %param.11) | copy-start | bytes 9437188
  2.5 116.6 %all-to-all-start = ((bf16[32,256,128]{1,2,0:T(8,128)(2,1)}), bf16[32,256,128]{1,2,0:T(8,128)(2,1)}, u32[]{:S(2)}, u32[]{:S(2)}) async-start(bf16[32,256,128]{1,2,0:T(8,128)(2,1)} %stack.2), calls=%async_computation | async-start | bytes 4194304 | tf_op jit(solution)/shard_map/all_to_all | solution.py:33
  19.1 2.9 copy-start.1
  19.1 2.9 copy-start.2
  123.0 66.2 %collective-permute-start.1 = (bf16[2,3,128]{2,1,0:T(4,128)(2,1)S(1)}, bf16[2,3,128]{2,1,0:T(4,128)(2,1)S(1)}, u32[]{:S(2)}, u32[]{:S(2)}) collective-permute-start(bf16[2,3,128]{2,1,0:T(4,128)(2,1)S(1)} %slice.35), channel_id=1, source_target_pairs={{0,32},{32,64},{64,96},{96,128},{128,160},{160,192},{192,224},{224... | collective-permute-start | bytes 4616 | tf_op jit(solution)/shard_map/ppermute | solution.py:11
  192.1 7.4 %collective-permute-start = (f32[16,128]{1,0:T(8,128)S(1)}, f32[16,128]{1,0:T(8,128)S(1)}, u32[]{:S(2)}, u32[]{:S(2)}) collective-permute-start(f32[16,128]{1,0:T(8,128)S(1)} %multiply_add_fusion.3), channel_id=1, source_target_pairs={{0,32},{32,64},{64,96},{96,128},{128,160},{160,192},{192,224},{224... | collective-permute-start | bytes 24584 | tf_op jit(solution)/shard_map/while/body/eval_jaxpr/ppermute | solution.py:11
  199.5 7.4 %collective-permute-start = (f32[16,128]{1,0:T(8,128)S(1)}, f32[16,128]{1,0:T(8,128)S(1)}, u32[]{:S(2)}, u32[]{:S(2)}) collective-permute-start(f32[16,128]{1,0:T(8,128)S(1)} %multiply_add_fusion.3), channel_id=1, source_target_pairs={{0,32},{32,64},{64,96},{96,128},{128,160},{160,192},{192,224},{224... | collective-permute-start | bytes 24584 | tf_op jit(solution)/shard_map/while/body/eval_jaxpr/ppermute | solution.py:11
  206.9 7.4 %collective-permute-start = (f32[16,128]{1,0:T(8,128)S(1)}, f32[16,128]{1,0:T(8,128)S(1)}, u32[]{:S(2)}, u32[]{:S(2)}) collective-permute-start(f32[16,128]{1,0:T(8,128)S(1)} %multiply_add_fusion.3), channel_id=1, source_target_pairs={{0,32},{32,64},{64,96},{96,128},{128,160},{160,192},{192,224},{224... | collective-permute-start | bytes 24584 | tf_op jit(solution)/shard_map/while/body/eval_jaxpr/ppermute | solution.py:11
  214.2 7.4 %collective-permute-start = (f32[16,128]{1,0:T(8,128)S(1)}, f32[16,128]{1,0:T(8,128)S(1)}, u32[]{:S(2)}, u32[]{:S(2)}) collective-permute-start(f32[16,128]{1,0:T(8,128)S(1)} %multiply_add_fusion.3), channel_id=1, source_target_pairs={{0,32},{32,64},{64,96},{96,128},{128,160},{160,192},{192,224},{224... | collective-permute-start | bytes 24584 | tf_op jit(solution)/shard_map/while/body/eval_jaxpr/ppermute | solution.py:11
  221.6 7.4 %collective-permute-start = (f32[16,128]{1,0:T(8,128)S(1)}, f32[16,128]{1,0:T(8,128)S(1)}, u32[]{:S(2)}, u32[]{:S(2)}) collective-permute-start(f32[16,128]{1,0:T(8,128)S(1)} %multiply_add_fusion.3), channel_id=1, source_target_pairs={{0,32},{32,64},{64,96},{96,128},{128,160},{160,192},{192,224},{224... | collective-permute-start | bytes 24584 | tf_op jit(solution)/shard_map/while/body/eval_jaxpr/ppermute | solution.py:11
  229.0 7.4 %collective-permute-start = (f32[16,128]{1,0:T(8,128)S(1)}, f32[16,128]{1,0:T(8,128)S(1)}, u32[]{:S(2)}, u32[]{:S(2)}) collective-permute-start(f32[16,128]{1,0:T(8,128)S(1)} %multiply_add_fusion.3), channel_id=1, source_target_pairs={{0,32},{32,64},{64,96},{96,128},{128,160},{160,192},{192,224},{224... | collective-permute-start | bytes 24584 | tf_op jit(solution)/shard_map/while/body/eval_jaxpr/ppermute | solution.py:11
  236.3 7.4 %collective-permute-start = (f32[16,128]{1,0:T(8,128)S(1)}, f32[16,128]{1,0:T(8,128)S(1)}, u32[]{:S(2)}, u32[]{:S(2)}) collective-permute-start(f32[16,128]{1,0:T(8,128)S(1)} %multiply_add_fusion.3), channel_id=1, source_target_pairs={{0,32},{32,64},{64,96},{96,128},{128,160},{160,192},{192,224},{224... | collective-permute-start | bytes 24584 | tf_op jit(solution)/shard_map/while/body/eval_jaxpr/ppermute | solution.py:11
  243.7 7.4 %collective-permute-start = (f32[16,128]{1,0:T(8,128)S(1)}, f32[16,128]{1,0:T(8,128)S(1)}, u32[]{:S(2)}, u32[]{:S(2)}) collective-permute-start(f32[16,128]{1,0:T(8,128)S(1)} %multiply_add_fusion.3), channel_id=1, source_target_pairs={{0,32},{32,64},{64,96},{96,128},{128,160},{160,192},{192,224},{224... | collective-permute-start | bytes 24584 | tf_op jit(solution)/shard_map/while/body/eval_jaxpr/ppermute | solution.py:11
  251.1 7.4 %collective-permute-start = (f32[16,128]{1,0:T(8,128)S(1)}, f32[16,128]{1,0:T(8,128)S(1)}, u32[]{:S(2)}, u32[]{:S(2)}) collective-permute-start(f32[16,128]{1,0:T(8,128)S(1)} %multiply_add_fusion.3), channel_id=1, source_target_pairs={{0,32},{32,64},{64,96},{96,128},{128,160},{160,192},{192,224},{224... | collective-permute-start | bytes 24584 | tf_op jit(solution)/shard_map/while/body/eval_jaxpr/ppermute | solution.py:11
  258.4 7.4 %collective-permute-start = (f32[16,128]{1,0:T(8,128)S(1)}, f32[16,128]{1,0:T(8,128)S(1)}, u32[]{:S(2)}, u32[]{:S(2)}) collective-permute-start(f32[16,128]{1,0:T(8,128)S(1)} %multiply_add_fusion.3), channel_id=1, source_target_pairs={{0,32},{32,64},{64,96},{96,128},{128,160},{160,192},{192,224},{224... | collective-permute-start | bytes 24584 | tf_op jit(solution)/shard_map/while/body/eval_jaxpr/ppermute | solution.py:11
  265.8 7.4 %collective-permute-start = (f32[16,128]{1,0:T(8,128)S(1)}, f32[16,128]{1,0:T(8,128)S(1)}, u32[]{:S(2)}, u32[]{:S(2)}) collective-permute-start(f32[16,128]{1,0:T(8,128)S(1)} %multiply_add_fusion.3), channel_id=1, source_target_pairs={{0,32},{32,64},{64,96},{96,128},{128,160},{160,192},{192,224},{224... | collective-permute-start | bytes 24584 | tf_op jit(solution)/shard_map/while/body/eval_jaxpr/ppermute | solution.py:11
  273.2 7.4 %collective-permute-start = (f32[16,128]{1,0:T(8,128)S(1)}, f32[16,128]{1,0:T(8,128)S(1)}, u32[]{:S(2)}, u32[]{:S(2)}) collective-permute-start(f32[16,128]{1,0:T(8,128)S(1)} %multiply_add_fusion.3), channel_id=1, source_target_pairs={{0,32},{32,64},{64,96},{96,128},{128,160},{160,192},{192,224},{224... | collective-permute-start | bytes 24584 | tf_op jit(solution)/shard_map/while/body/eval_jaxpr/ppermute | solution.py:11
  280.5 7.4 %collective-permute-start = (f32[16,128]{1,0:T(8,128)S(1)}, f32[16,128]{1,0:T(8,128)S(1)}, u32[]{:S(2)}, u32[]{:S(2)}) collective-permute-start(f32[16,128]{1,0:T(8,128)S(1)} %multiply_add_fusion.3), channel_id=1, source_target_pairs={{0,32},{32,64},{64,96},{96,128},{128,160},{160,192},{192,224},{224... | collective-permute-start | bytes 24584 | tf_op jit(solution)/shard_map/while/body/eval_jaxpr/ppermute | solution.py:11
  287.9 7.4 %collective-permute-start = (f32[16,128]{1,0:T(8,128)S(1)}, f32[16,128]{1,0:T(8,128)S(1)}, u32[]{:S(2)}, u32[]{:S(2)}) collective-permute-start(f32[16,128]{1,0:T(8,128)S(1)} %multiply_add_fusion.3), channel_id=1, source_target_pairs={{0,32},{32,64},{64,96},{96,128},{128,160},{160,192},{192,224},{224... | collective-permute-start | bytes 24584 | tf_op jit(solution)/shard_map/while/body/eval_jaxpr/ppermute | solution.py:11
  295.3 7.4 %collective-permute-start = (f32[16,128]{1,0:T(8,128)S(1)}, f32[16,128]{1,0:T(8,128)S(1)}, u32[]{:S(2)}, u32[]{:S(2)}) collective-permute-start(f32[16,128]{1,0:T(8,128)S(1)} %multiply_add_fusion.3), channel_id=1, source_target_pairs={{0,32},{32,64},{64,96},{96,128},{128,160},{160,192},{192,224},{224... | collective-permute-start | bytes 24584 | tf_op jit(solution)/shard_map/while/body/eval_jaxpr/ppermute | solution.py:11
  304.2 15.4 %copy-start.3 = (f32[128]{0:T(128)S(1)}, f32[128]{0:T(128)}, u32[]{:S(2)}) copy-start(f32[128]{0:T(128)} %param.15) | copy-start | bytes 1540
